TPU v7x, 32 devices: a whole 2x2x4 slice. The times are simulated.
32 devices in a mesh: batch: 8 (over z, x), tok: 4 (over y, core).
Axes of the slice: x: 2, y: 2, z: 4, core: 2. Of those that a mesh axis runs over, the one named last changes fastest.
Arguments:
- patches: bfloat16 [24, 1024, 768], P('batch', 'tok'), may hold values from -6 to 6
- image_ids: int32 [24, 1024], P('batch', 'tok'), may hold values from -1 to 3, as said below
- cotangent: bfloat16 [24, 1024, 768], P('batch', 'tok'), may hold values from -6 to 6
- norm_gain: float32 [768], replicated, may hold values from 0.25 to 1.75
- query_gain: float32 [64], replicated, may hold values from 0.25 to 1.75
- key_gain: float32 [64], replicated, may hold values from 0.25 to 1.75
- in_weight: bfloat16 [768, 5376], P(('batch', 'tok')), may hold values from -0.21875 to 0.21875
- out_weight: bfloat16 [3840, 768], P(('batch', 'tok')), may hold values from -0.6538492 to 0.6538492
Outputs:
- block_out: bfloat16 [24, 1024, 768], P('batch', 'tok')
- patch_grad: bfloat16 [24, 1024, 768], P('batch', 'tok')
- norm_grad: float32 [768], replicated
- query_grad: float32 [64], replicated
- key_grad: float32 [64], replicated
- in_grad: float32 [768, 5376], P(('batch', 'tok'))
- out_grad: float32 [3840, 768], P(('batch', 'tok'))
Inputs may be any that keep to these rules, and one draw needn't show every extreme that they name: `image_ids`: in each sequence the ids of the live tokens run 0, 1, 2, 3 in contiguous non-decreasing runs (a run may be empty; the last image is never empty), followed by at least one padding slot of -1 at the end of the sequence.
All inputs are finite; a program needn't handle non-finite values.
Results may differ from a plain program's by a relative error of at most 0.0097.
Values may be sent and summed in bfloat16 or wider, within the bound.
No kernel may reach another device: no remote copies, remote signals or barrier semaphores. Data moves between devices by JAX's collectives and lax.ppermute only.
A program may use at most 192 MiB of HBM per device.

v0:
```python
import math
import jax
import jax.numpy as jnp
from jax import lax
from jax.sharding import PartitionSpec as P

H = 12
HD = 64
mask_fill = -1000000000.0
norm_eps = 1e-06


def normalize(values):
    center = values - jnp.mean(values, axis=-1, keepdims=True)
    inverse = lax.rsqrt(jnp.mean(center * center, axis=-1, keepdims=True) + norm_eps)
    return (center * inverse, inverse)


def norm_back(grad_unit, unit_rows, inverse):
    return inverse * (
        grad_unit
        - jnp.mean(grad_unit, axis=-1, keepdims=True)
        - unit_rows * jnp.mean(grad_unit * unit_rows, axis=-1, keepdims=True)
    )


def head_scores(query_block, key_block, seq_ids):
    score_scale = 1.0 / math.sqrt(query_block.shape[-1])
    scores = (
        jnp.einsum("qhd,khd->hqk", query_block, key_block, preferred_element_type=jnp.float32)
        * score_scale
    )
    allowed = (seq_ids[:, None] == seq_ids[None, :]) & (seq_ids[:, None] >= 0)
    return jnp.where(allowed[None], scores, mask_fill)


def forward_sequence(inputs):
    query_block, key_block, value_block, seq_ids = inputs
    scores = head_scores(query_block, key_block, seq_ids)
    row_max = jnp.max(scores, axis=-1, keepdims=True)
    weights = jnp.exp(scores - row_max)
    row_total = jnp.sum(weights, axis=-1, keepdims=True)
    probabilities = (weights / row_total).astype(jnp.bfloat16)
    outputs = jnp.einsum(
        "hqk,khd->qhd", probabilities, value_block, preferred_element_type=jnp.float32
    )
    return (outputs.astype(jnp.bfloat16), (row_max + jnp.log(row_total))[..., 0])


def backward_sequence(inputs):
    query_block, key_block, value_block, seq_ids, log_total, grad_out = inputs
    score_scale = 1.0 / math.sqrt(query_block.shape[-1])
    scores = head_scores(query_block, key_block, seq_ids)
    probabilities = jnp.exp(scores - log_total[..., None])
    grad_probs = jnp.einsum(
        "qhd,khd->hqk", grad_out, value_block, preferred_element_type=jnp.float32
    )
    weighted = jnp.sum(probabilities * grad_probs, axis=-1, keepdims=True)
    grad_scores = (probabilities * (grad_probs - weighted)).astype(jnp.bfloat16)
    grad_query = score_scale * jnp.einsum(
        "hqk,khd->qhd", grad_scores, key_block, preferred_element_type=jnp.float32
    )
    grad_key = score_scale * jnp.einsum(
        "hqk,qhd->khd", grad_scores, query_block, preferred_element_type=jnp.float32
    )
    grad_value = jnp.einsum(
        "hqk,qhd->khd",
        probabilities.astype(jnp.bfloat16),
        grad_out,
        preferred_element_type=jnp.float32,
    )
    return (
        grad_query.astype(jnp.bfloat16),
        grad_key.astype(jnp.bfloat16),
        grad_value.astype(jnp.bfloat16),
    )


def per_device(
    patches, image_ids, cotangent, norm_gain, query_gain, key_gain, in_weight, out_weight
):
    seq_count, part_len, feature_width = patches.shape
    row_count = seq_count * part_len
    contract_last = (((1,), (1,)), ((), ()))
    contract_first = (((0,), (0,)), ((), ()))
    live_rows = (image_ids >= 0).astype(jnp.float32).reshape(row_count, 1)
    flat_rows = patches.reshape(row_count, feature_width).astype(jnp.float32)
    unit_rows, inverse = normalize(flat_rows)
    normed = (unit_rows * norm_gain).astype(jnp.bfloat16)
    in_full = lax.all_gather(in_weight, ("batch", "tok"), axis=0, tiled=True)
    merged = jnp.dot(normed, in_full, preferred_element_type=jnp.float32)
    query_unit, query_inverse = normalize(merged[:, :feature_width].reshape(row_count, H, HD))
    key_unit, key_inverse = normalize(
        merged[:, feature_width : 2 * feature_width].reshape(row_count, H, HD)
    )
    head_shape = (seq_count, part_len, H, HD)
    queries = (query_unit * query_gain).astype(jnp.bfloat16).reshape(head_shape)
    key_rows = (key_unit * key_gain).astype(jnp.bfloat16).reshape(head_shape)
    value_rows = (
        merged[:, 2 * feature_width : 3 * feature_width].astype(jnp.bfloat16).reshape(head_shape)
    )
    up_proj = merged[:, 3 * feature_width :]
    hidden = jax.nn.gelu(up_proj).astype(jnp.bfloat16)
    ids_full = lax.all_gather(image_ids, "tok", axis=1, tiled=True)
    query_heads, key_heads, value_heads = (
        lax.all_to_all(queries, "tok", split_axis=2, concat_axis=1, tiled=True),
        lax.all_to_all(key_rows, "tok", split_axis=2, concat_axis=1, tiled=True),
        lax.all_to_all(value_rows, "tok", split_axis=2, concat_axis=1, tiled=True),
    )
    heads_out, log_total = lax.map(
        forward_sequence, (query_heads, key_heads, value_heads, ids_full)
    )
    heads_tok = lax.all_to_all(heads_out, "tok", split_axis=1, concat_axis=2, tiled=True)
    combined = jnp.concatenate([heads_tok.reshape(row_count, feature_width), hidden], axis=1)
    out_full = lax.all_gather(out_weight, ("batch", "tok"), axis=0, tiled=True)
    branch = jnp.dot(combined, out_full, preferred_element_type=jnp.float32)
    block_out = (
        (live_rows * (flat_rows + branch))
        .astype(jnp.bfloat16)
        .reshape(seq_count, part_len, feature_width)
    )
    grad_branch = (
        live_rows * cotangent.reshape(row_count, feature_width).astype(jnp.float32)
    ).astype(jnp.bfloat16)
    out_back = lax.all_gather(out_weight, ("batch", "tok"), axis=0, tiled=True)
    grad_combined = lax.dot_general(
        grad_branch, out_back, contract_last, preferred_element_type=jnp.float32
    )
    grad_heads = grad_combined[:, :feature_width].astype(jnp.bfloat16).reshape(head_shape)
    grad_hidden = grad_combined[:, feature_width:]
    grad_heads_h = lax.all_to_all(grad_heads, "tok", split_axis=2, concat_axis=1, tiled=True)
    grad_query_h, grad_key_h, grad_value_h = lax.map(
        backward_sequence, (query_heads, key_heads, value_heads, ids_full, log_total, grad_heads_h)
    )
    grad_query, grad_key, grad_value = (
        lax.all_to_all(grad_query_h, "tok", split_axis=1, concat_axis=2, tiled=True),
        lax.all_to_all(grad_key_h, "tok", split_axis=1, concat_axis=2, tiled=True),
        lax.all_to_all(grad_value_h, "tok", split_axis=1, concat_axis=2, tiled=True),
    )
    grad_query = grad_query.reshape(row_count, H, HD).astype(jnp.float32)
    grad_key = grad_key.reshape(row_count, H, HD).astype(jnp.float32)
    query_grad = jnp.sum(grad_query * query_unit, axis=(0, 1))
    key_grad = jnp.sum(grad_key * key_unit, axis=(0, 1))
    grad_query_raw = norm_back(grad_query * query_gain, query_unit, query_inverse).reshape(
        row_count, feature_width
    )
    grad_key_raw = norm_back(grad_key * key_gain, key_unit, key_inverse).reshape(
        row_count, feature_width
    )
    unused_value, gelu_pull = jax.vjp(jax.nn.gelu, up_proj)
    grad_up = gelu_pull(grad_hidden)[0]
    grad_merged = jnp.concatenate(
        [
            grad_query_raw,
            grad_key_raw,
            grad_value.reshape(row_count, feature_width).astype(jnp.float32),
            grad_up,
        ],
        axis=1,
    ).astype(jnp.bfloat16)
    in_back = lax.all_gather(in_weight, ("batch", "tok"), axis=0, tiled=True)
    grad_normed = lax.dot_general(
        grad_merged, in_back, contract_last, preferred_element_type=jnp.float32
    )
    columns = combined
    out_grad = lax.psum_scatter(
        lax.dot_general(columns, grad_branch, contract_first, preferred_element_type=jnp.float32),
        ("batch", "tok"),
        scatter_dimension=0,
        tiled=True,
    )
    columns = normed
    in_grad = lax.psum_scatter(
        lax.dot_general(columns, grad_merged, contract_first, preferred_element_type=jnp.float32),
        ("batch", "tok"),
        scatter_dimension=0,
        tiled=True,
    )
    norm_grad = jnp.sum(grad_normed * unit_rows, axis=0)
    norm_grad, query_grad, key_grad = lax.psum((norm_grad, query_grad, key_grad), ("batch", "tok"))
    input_grad = grad_branch.astype(jnp.float32) + norm_back(
        grad_normed * norm_gain, unit_rows, inverse
    )
    patch_grad = input_grad.astype(jnp.bfloat16).reshape(seq_count, part_len, feature_width)
    return (block_out, patch_grad, norm_grad, query_grad, key_grad, in_grad, out_grad)


def solution(mesh):
    return jax.shard_map(
        per_device,
        mesh=mesh,
        in_specs=(
            P("batch", "tok", None),
            P("batch", "tok"),
            P("batch", "tok", None),
            P(),
            P(),
            P(),
            P(("batch", "tok"), None),
            P(("batch", "tok"), None),
        ),
        out_specs=(
            P("batch", "tok", None),
            P("batch", "tok", None),
            P(),
            P(),
            P(),
            P(("batch", "tok"), None),
            P(("batch", "tok"), None),
        ),
        check_vma=False,
    )
```

profile of v0, /device:TPU:0, one launch (start us, length us, event | category | flops | bytes accessed | tf_op | source)
XLA Modules:
  0.0 865.3 jit_solution(12807134748747574468)
XLA Ops:
  13.2 68.2 %all-gather.5.cloned.1.call-done = bf16[3840,768]{1,0:T(8,128)(2,1)} async-done(((bf16[120,768]{1,0:T(8,128)(2,1)}), bf16[3840,768]{1,0:T(8,128)(2,1)}) %all-gather.5.cloned.1.call-update) | async-done | bytes 5898256 | tf_op jit(solution)/shard_map/all_gather | solution.py:115
  81.4 7.4 fusion.93
  100.5 4.4 all-to-all-start.4
  104.9 56.8 %all-gather.3.cloned.1.call-done = bf16[768,5376]{1,0:T(8,128)(2,1)} async-done(((bf16[24,5376]{1,0:T(8,128)(2,1)}), bf16[768,5376]{1,0:T(8,128)(2,1)}) %all-gather.3.cloned.1.call-update) | async-done | bytes 8257552 | tf_op jit(solution)/shard_map/all_gather | solution.py:90
  161.7 8.7 %fusion.92 = f32[768,5376]{1,0:T(8,128)S(1)} fusion(bf16[768,768]{1,0:T(8,128)(2,1)S(1)} %copy-done.15, bf16[768,5376]{1,0:T(8,128)(2,1)} %all-gather.3.cloned.1.call-done), kind=kOutput, calls=%fused_computation.141 | convolution fusion | flops 6341787648 | bytes 25952256 | tf_op jit(solution)/shard_map/dot_general | solution.py:91
  170.4 5.8 copy-done.1
  183.6 4.8 fusion.91
  191.3 15.2 %all-to-all-start = ((bf16[3,256,12,64]{1,3,0,2:T(8,128)(2,1)}), bf16[3,256,12,64]{1,3,0,2:T(8,128)(2,1)S(1)}, u32[]{:S(2)}, u32[]{:S(2)}) async-start(bf16[3,256,12,64]{1,3,0,2:T(8,128)(2,1)} %copy.166), calls=%async_computation | async-start | bytes 2359296 | tf_op jit(solution)/shard_map/all_to_all | solution.py:108
  237.3 4.9 all-to-all-done.1
  245.8 16.8 %all_gather.12 = s32[3,1024]{1,0:T(4,128)S(1)} all-gather(s32[3,256]{1,0:T(4,128)S(1)} %copy-done.32), channel_id=1, replica_groups=mesh['batch'=8,'tok'=4] {'tok'}, dimensions={1}, use_global_device_ids=true | all-gather | bytes 15360 | tf_op jit(solution)/shard_map/all_gather | solution.py:104
  276.7 45.7 %while.26 = (s32[]{:T(128)}, bf16[3,1024,3,64]{1,3,2,0:T(8,128)(2,1)}, f32[3,3,1024]{2,1,0:T(4,128)}, bf16[3,1024,3,64]{1,3,2,0:T(8,128)(2,1)}, s32[3,1024]{1,0:...) while((s32[]{:T(128)}, ...), condition=%wide.region_9.10_spmd, body=%wide.region_6.9_spmd.sunk | while | flops 845346816 | bytes 47833216 | solution.py:110
  285.6 5.7 fusion.123
  300.8 5.7 fusion.123
  316.1 5.7 fusion.123
  322.4 4.6 copy.179
  334.8 14.1 %fusion.65 = (bf16[768,3072]{1,0:T(8,128)(2,1)}, bf16[768,3072]{1,0:T(8,128)(2,1)}) fusion(f32[768,3840]{1,0:T(8,128)} %copy-done.7, f32[768,5376]{1,0:T(8,128)} %copy-done.1), kind=kLoop, calls=%fused_computation.76 | loop fusion | flops 51904512 | bytes 28311552 | tf_op jit(solution)/shard_map/convert.19
  360.2 11.9 %fusion.66 = f32[3840,768]{1,0:T(8,128)} fusion(bf16[768,768]{1,0:T(8,128)(2,1)S(1)} %copy-done.20, bf16[768,3072]{1,0:T(8,128)(2,1)} %get-tuple-element.157, bf16[768,768]{1,0:T(8,128)(2,1)S(1)} %copy.181), kind=kOutput, calls=%fused_computation.80 | convolution fusion | flops 4541644800 | bytes 18874368 | tf_op jit(solution)/shard_map/dot_general | solution.py:167
  375.8 84.0 %while.27 = (s32[]{:T(128)}, bf16[3,1024,3,64]{1,3,2,0:T(8,128)(2,1)}, bf16[3,1024,3,64]{1,3,2,0:T(8,128)(2,1)}, bf16[3,1024,3,64]{1,3,2,0:T(8,128)(2,1)}, bf16[...) while((s32[]{:T(128)}, ...), condition=%wide.region_12.13_spmd, body=%wide.region_10.12_spmd.sunk | while | flops 2063529984 | bytes 102616192 | solution.py:132
  379.3 8.3 multiply_reduce_fusion.11
  387.6 7.5 multiply_convert_fusion.7
  399.9 4.4 fusion.135
  407.6 8.3 multiply_reduce_fusion.11
  415.9 6.9 multiply_convert_fusion.7
  427.6 4.4 fusion.135
  435.4 8.3 multiply_reduce_fusion.11
  443.6 7.0 multiply_convert_fusion.7
  459.8 4.6 copy.216
  471.8 4.6 copy.186
  479.5 18.2 %all-to-all-done.7 = bf16[4,2,73728]{2,1,0:T(2,128)(2,1)} async-done(((bf16[4,2,73728]{2,1,0:T(2,128)(2,1)}), bf16[4,2,73728]{2,1,0:T(2,128)(2,1)}, u32[]{:S(2)}, u32[]{:S(2)}) %all-to-all-start.7) | async-done | bytes 1179680 | tf_op jit(solution)/shard_map/all_to_all | solution.py:138
  497.7 4.5 all-to-all-start.5
  502.3 4.6 copy.201
  510.0 10.8 %all-to-all-done.5 = bf16[4,2,73728]{2,1,0:T(2,128)(2,1)} async-done(((bf16[4,2,73728]{2,1,0:T(2,128)(2,1)}), bf16[4,2,73728]{2,1,0:T(2,128)(2,1)}, u32[]{:S(2)}, u32[]{:S(2)}) %all-to-all-start.5) | async-done | bytes 1179680 | tf_op jit(solution)/shard_map/all_to_all | solution.py:136
  525.3 7.9 reshape.416
  533.3 5.4 reshape.418
  540.9 6.6 copy.196
  551.8 6.5 copy.211
  581.2 4.9 multiply_reduce_fusion.2
  595.6 5.0 copy.231
  600.6 8.1 reshape.415
  618.6 4.9 multiply_reduce_fusion.1
  633.0 5.0 copy.234
  638.0 7.8 reshape.417
  645.8 9.4 %multiply_convert_fusion.5 = (bf16[768,768]{1,0:T(8,128)(2,1)S(1)}, bf16[768,768]{1,0:T(8,128)(2,1)S(1)}) fusion(f32[768,768]{1,0:T(8,128)S(1)} %copy-done.8, f32[768,768]{1,0:T(8,128)} %copy.199, f32[768,768]{1,0:T(8,128)} %copy.192, f32[768,768]{1,0:T(8,128)} %copy.191, f32[768,768]{1,0:T(8,128)} %reshape.415, f32[768]{0:T(1024)S(1)} %mul.317, ...), kind=kLoop, calls=%fused_computation.113 | loop fusion | flops 9437184 | bytes 30676992 | tf_op jit(solution)/shard_map/convert.16
  656.3 12.3 %fusion.85 = f32[768,5376]{1,0:T(8,128)} fusion(bf16[768,768]{1,0:T(8,128)(2,1)S(1)} %copy-done.16, bf16[768,3072]{1,0:T(8,128)(2,1)} %get-tuple-element.156, bf16[768,768]{1,0:T(8,128)(2,1)S(1)} %copy-done.21, bf16[768,768]{1,0:T(8,128)(2,1)S(1)} %get-tuple-element.155, bf16[768,768]{1,0:T(8,128)(2,1)S(1)} %get-tuple-element.154), kind=kOutput, calls=%fused_computation.121 | convolution fusion | flops 6374817792 | bytes 25952256 | tf_op jit(solution)/shard_map/dot_general | solution.py:174
  669.9 13.3 %fusion.82 = (f32[768]{0:T(1024)}, f32[768]{0:T(1024)}, f32[768]{0:T(1024)}, f32[768,768]{1,0:T(8,128)}) fusion(bf16[3,256,768]{2,1,0:T(8,128)(2,1)S(1)} %copy-done.6, f32[768]{0:T(1024)S(1)} %copy-done.31, f32[768]{0:T(1024)S(1)} %copy-done.29, f32[768]{0:T(1024)S(1)} %copy-done.34, bf16[768,5376]{1,0:T(8,128)(2,1)} %all-gather.3.cloned.1.call-done, ...), kind=kOutput, calls=%fused_computation.105 | convolution fusion | flops 6380123136 | bytes 20072448 | tf_op jit(solution)/shard_map/dot_general | solution.py:162
  683.2 40.7 %all-reduce = (f32[768]{0:T(1024)}, f32[64]{0:T(128)}, f32[64]{0:T(128)}) all-reduce(f32[768]{0:T(1024)} %get-tuple-element.108, f32[64]{0:T(128)} %get-tuple-element.106, f32[64]{0:T(128)} %get-tuple-element.104), channel_id=1, replica_groups=mesh['batch'=8,'tok'=4] {'batch','tok'}, use_global_device_ids=true, to_apply=%region_20.21 | all-reduce | flops 896 | bytes 7168 | tf_op jit(solution)/shard_map/psum | solution.py:180
  729.0 9.9 %fusion.84 = bf16[768,768]{1,0:T(8,128)(2,1)} fusion(bf16[3,256,768]{2,1,0:T(8,128)(2,1)S(1)} %copy-done.6, bf16[3840,768]{1,0:T(8,128)(2,1)} %all-gather.5.cloned.1.call-done, bf16[768,3072]{1,0:T(8,128)(2,1)} %get-tuple-element.157, bf16[768,768]{1,0:T(8,128)(2,1)S(1)} %copy-done.18, f32[768]{0:T(1024)S(1)} %copy-done.27), kind=kOutput, calls=%fused_computation.107 | convolution fusion | flops 4544004096 | bytes 14158848 | tf_op jit(solution)/shard_map/dot_general | solution.py:116
  738.9 119.7 %reduce-scatter.3.cloned.1.call-done = f32[24,5376]{1,0:T(8,128)} async-done(((f32[768,5376]{1,0:T(8,128)}), f32[24,5376]{1,0:T(8,128)}) %reduce-scatter.3.cloned.1.call-update) | async-done | bytes 516112 | tf_op jit(solution)/shard_map/reduce_scatter | solution.py:173
  (252 shorter events, 239.8 us)
Async XLA Ops:
  7.2 3.8 copy-start.5
  7.2 4.2 copy-start.10
  7.2 74.2 %all-gather.5.cloned.1.call-start = ((), (), s32[]{:S(2)}) async-start(), calls=%async_computation.11 | async-start | bytes 6082560 | tf_op jit(solution)/shard_map/all_gather | solution.py:115
  7.9 153.7 %all-gather.3.cloned.1.call-start = ((), (), s32[]{:S(2)}) async-start(), calls=%async_computation.10 | async-start | bytes 8515584 | tf_op jit(solution)/shard_map/all_gather | solution.py:90
  9.4 2.4 copy-start.26
  9.4 2.4 copy-start.33
  10.9 2.3 copy-start.28
  11.4 1.8 copy-start.30
  11.8 77.1 %copy-start.19 = (bf16[768,768]{1,0:T(8,128)(2,1)}, bf16[768,768]{1,0:T(8,128)(2,1)S(1)}, u32[]{:S(2)}) copy-start(bf16[768,768]{1,0:T(8,128)(2,1)S(1)} %fusion.68) | copy-start | bytes 3538948
  88.8 4.3 copy-start.7
  100.5 61.2 %copy-start.15 = (bf16[768,768]{1,0:T(8,128)(2,1)S(1)}, bf16[768,768]{1,0:T(8,128)(2,1)}, u32[]{:S(2)}) copy-start(bf16[768,768]{1,0:T(8,128)(2,1)} %fusion.76) | copy-start | bytes 3538948
  100.5 90.8 %all-to-all-start.4 = ((bf16[3,256,12,64]{1,3,0,2:T(8,128)(2,1)}), bf16[3,256,12,64]{1,3,0,2:T(8,128)(2,1)}, u32[]{:S(2)}, u32[]{:S(2)}) async-start(bf16[3,256,12,64]{1,3,0,2:T(8,128)(2,1)} %copy.183), calls=%async_computation.4 | async-start | bytes 2359296 | tf_op jit(solution)/shard_map/all_to_all | solution.py:131
  170.4 5.8 copy-start.1
  191.3 30.8 %all-to-all-start = ((bf16[3,256,12,64]{1,3,0,2:T(8,128)(2,1)}), bf16[3,256,12,64]{1,3,0,2:T(8,128)(2,1)S(1)}, u32[]{:S(2)}, u32[]{:S(2)}) async-start(bf16[3,256,12,64]{1,3,0,2:T(8,128)(2,1)} %copy.166), calls=%async_computation | async-start | bytes 2359296 | tf_op jit(solution)/shard_map/all_to_all | solution.py:108
  210.7 2.6 copy-start.35
  213.3 3.0 copy-start.22
  222.1 20.2 %all-to-all-start.1 = ((bf16[3,256,12,64]{1,3,0,2:T(8,128)(2,1)}), bf16[3,256,12,64]{1,3,0,2:T(8,128)(2,1)}, u32[]{:S(2)}, u32[]{:S(2)}) async-start(bf16[3,256,12,64]{1,3,0,2:T(8,128)(2,1)} %copy.171), calls=%async_computation.1 | async-start | bytes 2359296 | tf_op jit(solution)/shard_map/all_to_all | solution.py:106
  230.5 2.6 copy-start.37
  233.1 3.0 copy-start.24
  236.1 9.8 %copy-start.32 = (s32[3,256]{1,0:T(4,128)S(1)}, s32[3,256]{1,0:T(4,128)}, u32[]{:S(2)}) copy-start(s32[3,256]{1,0:T(4,128)} %param.13) | copy-start | bytes 9220
  242.3 30.7 %all-to-all-start.2 = ((bf16[3,256,12,64]{1,3,0,2:T(8,128)(2,1)}), bf16[3,256,12,64]{1,3,0,2:T(8,128)(2,1)S(1)}, u32[]{:S(2)}, u32[]{:S(2)}) async-start(bf16[3,256,12,64]{1,3,0,2:T(8,128)(2,1)} %copy.176), calls=%async_computation.2 | async-start | bytes 2359296 | tf_op jit(solution)/shard_map/all_to_all | solution.py:107
  277.5 4.3 copy-start
  292.7 4.3 copy-start
  307.9 4.3 copy-start
  330.0 20.2 %all-to-all-start.3 = ((bf16[4,2,73728]{2,1,0:T(2,128)(2,1)}), bf16[4,2,73728]{2,1,0:T(2,128)(2,1)}, u32[]{:S(2)}, u32[]{:S(2)}) async-start(bf16[4,2,73728]{2,1,0:T(2,128)(2,1)} %reshape.419), calls=%async_computation.3 | async-start | bytes 2359296 | tf_op jit(solution)/shard_map/all_to_all | solution.py:113
  334.3 404.6 %reduce-scatter.5.cloned.1.call-start = ((), (), s32[]{:S(2)}) async-start(), calls=%async_computation.13 | async-start | bytes 12165120 | tf_op jit(solution)/shard_map/reduce_scatter | solution.py:166
  357.8 2.5 copy-start.20
  360.2 11.9 %copy-start.17 = (bf16[768,768]{1,0:T(8,128)(2,1)}, bf16[768,768]{1,0:T(8,128)(2,1)S(1)}, u32[]{:S(2)}) copy-start(bf16[768,768]{1,0:T(8,128)(2,1)S(1)} %copy.181) | copy-start | bytes 3538948
  372.1 3.6 copy-start.2
  372.2 3.6 copy-start.3
  372.2 3.6 copy-start.9
  467.5 30.2 %all-to-all-start.7 = ((bf16[4,2,73728]{2,1,0:T(2,128)(2,1)}), bf16[4,2,73728]{2,1,0:T(2,128)(2,1)}, u32[]{:S(2)}, u32[]{:S(2)}) async-start(bf16[4,2,73728]{2,1,0:T(2,128)(2,1)} %reshape.421), calls=%async_computation.7 | async-start | bytes 2359296 | tf_op jit(solution)/shard_map/all_to_all | solution.py:138
  497.7 23.1 %all-to-all-start.5 = ((bf16[4,2,73728]{2,1,0:T(2,128)(2,1)}), bf16[4,2,73728]{2,1,0:T(2,128)(2,1)}, u32[]{:S(2)}, u32[]{:S(2)}) async-start(bf16[4,2,73728]{2,1,0:T(2,128)(2,1)} %reshape.425), calls=%async_computation.5 | async-start | bytes 2359296 | tf_op jit(solution)/shard_map/all_to_all | solution.py:136
  506.9 18.3 %copy-start.36 = (f32[64]{0:T(128)S(1)}, f32[64]{0:T(128)}, u32[]{:S(2)}) copy-start(f32[64]{0:T(128)} %param.16) | copy-start | bytes 772
  506.9 18.4 %copy-start.38 = (f32[64]{0:T(128)S(1)}, f32[64]{0:T(128)}, u32[]{:S(2)}) copy-start(f32[64]{0:T(128)} %param.17) | copy-start | bytes 772
  520.8 87.8 %all-to-all-start.6 = ((bf16[4,2,73728]{2,1,0:T(2,128)(2,1)}), bf16[4,2,73728]{2,1,0:T(2,128)(2,1)}, u32[]{:S(2)}, u32[]{:S(2)}) async-start(bf16[4,2,73728]{2,1,0:T(2,128)(2,1)} %reshape.423), calls=%async_computation.6 | async-start | bytes 2359296 | tf_op jit(solution)/shard_map/all_to_all | solution.py:137
  525.1 333.5 %reduce-scatter.3.cloned.1.call-start = ((), (), s32[]{:S(2)}) async-start(), calls=%async_computation.12 | async-start | bytes 17031168 | tf_op jit(solution)/shard_map/reduce_scatter | solution.py:173
  525.3 7.9 copy-start.23
  525.3 7.9 copy-start.12
  525.3 7.9 copy-start.4
  533.2 5.5 copy-start.25
  533.3 5.5 copy-start.13
  638.0 7.8 copy-start.8
  645.8 10.5 %copy-start.16 = (bf16[768,768]{1,0:T(8,128)(2,1)S(1)}, bf16[768,768]{1,0:T(8,128)(2,1)}, u32[]{:S(2)}) copy-start(bf16[768,768]{1,0:T(8,128)(2,1)} %fusion.76) | copy-start | bytes 3538948
  645.8 10.5 %copy-start.21 = (bf16[768,768]{1,0:T(8,128)(2,1)S(1)}, bf16[768,768]{1,0:T(8,128)(2,1)}, u32[]{:S(2)}) copy-start(bf16[768,768]{1,0:T(8,128)(2,1)} %copy.218) | copy-start | bytes 3538948
  669.8 55.4 %copy-start.11 = (bf16[3,256,768]{2,1,0:T(8,128)(2,1)S(1)}, bf16[3,256,768]{2,1,0:T(8,128)(2,1)}, u32[]{:S(2)}) copy-start(bf16[3,256,768]{2,1,0:T(8,128)(2,1)} %param.14) | copy-start | bytes 3538948
  669.9 55.4 %copy-start.27 = (f32[768]{0:T(1024)S(1)}, f32[768]{0:T(1024)}, u32[]{:S(2)}) copy-start(f32[768]{0:T(1024)} %copy-done.26) | copy-start | bytes 9220
  725.3 3.7 copy-start.18
  (5 other events, 6.1 us)
Sparse Core Ops, SparseCore 0:
  10.9 70.3 all-gather.4
  84.3 77.3 all-gather.2
  372.3 156.6 reduce-scatter.4
  668.7 189.7 reduce-scatter.2
where the time goes:
time: 876 us; the launch traced here: 865 us
  waiting for transfers between devices  283 us (32%)
  local copies, waits for them, and re-layouts  218 us (25%)
  matrix products  151 us (17%)
  other arithmetic  94.8 us (11%)
  blocking collectives  57.5 us (7%)
  starting transfers between devices  45.3 us (5%)
  between operations  14.8 us (2%)
    reduce_scatter x1, waiting for transfers between devices, per_device(): lax.psum_scatter(lax.dot_general(columns, grad_merged, contract_first, pr...  120 us
    all_gather x1, waiting for transfers between devices, per_device(): out_full = lax.all_gather(out_weight, ('batch', 'tok'), axis=0, tiled=True)  68.2 us
    all_gather x1, waiting for transfers between devices, per_device(): in_full = lax.all_gather(in_weight, ('batch', 'tok'), axis=0, tiled=True)  56.8 us
    unnamed x94, local copies, waits for them, and re-layouts  42.2 us
    psum x1, blocking collectives, per_device(): lax.psum((norm_grad, query_grad, key_grad), ('batch', 'tok'))  40.7 us
    dot_general x3, matrix products, backward_sequence(): jnp.einsum('qhd,khd->hqk', grad_out, value_block, preferred_element_type=...  24.8 us
    another operation x2, other arithmetic  23.5 us
    convert_element_type x3, other arithmetic, backward_sequence(): grad_scores = (probabilities * (grad_probs - weighted)).astype(jnp.bfloat16)  21.5 us
  transfers between devices with their start and end apart: 12, of which 8 were waited for; matrix products, arithmetic and copies ran while one was open for 43% of the time, Pallas kernels for 0%

commit v1 on v0

--- a/solution.py
+++ b/solution.py
@@ -133,7 +133,12 @@
         backward_sequence, (query_heads, key_heads, value_heads, ids_full, log_total, grad_heads_h)
     )
     grad_query, grad_key, grad_value = (
-        lax.all_to_all(grad_query_h, "tok", split_axis=1, concat_axis=2, tiled=True),
+        jnp.concatenate(
+            lax.all_to_all(
+                jnp.stack(jnp.split(grad_query_h, lax.axis_size("tok"), axis=1)), "tok", 0, 0
+            ),
+            axis=2,
+        ),
         lax.all_to_all(grad_key_h, "tok", split_axis=1, concat_axis=2, tiled=True),
         lax.all_to_all(grad_value_h, "tok", split_axis=1, concat_axis=2, tiled=True),
     )

time: 876 us -> 849 us (0.969)
  local copies, waits for them, and re-layouts: 218 us -> 198 us
  starting transfers between devices: 45.3 us -> 33.4 us
    all_to_all x1, starting transfers between devices: 15.2 us -> 3.99 us  [per_device(): lax.all_to_all(value_rows, 'tok', split_axis=2, concat_axis=1, tiled=True)]
    unnamed x94 -> x102, local copies, waits for them, and re-layouts: 42.2 us -> 35.8 us
    another operation x2 -> x3, other arithmetic: 23.5 us -> 24.7 us
  transfers between devices with their start and end apart: 12 -> 12, of which waited for: 8 -> 8; matrix products, arithmetic and copies ran while one was open for 43% -> 42% of each run, Pallas kernels for 0% -> 0%
where the time goes in v1:
time: 849 us; the launch traced here: 838 us
  waiting for transfers between devices  288 us (34%)
  local copies, waits for them, and re-layouts  198 us (23%)
  matrix products  151 us (18%)
  other arithmetic  95.6 us (11%)
  blocking collectives  57.6 us (7%)
  starting transfers between devices  33.4 us (4%)
  between operations  14.8 us (2%)
    reduce_scatter x1, waiting for transfers between devices, per_device(): lax.psum_scatter(lax.dot_general(columns, grad_merged, contract_first, pr...  119 us
    all_gather x1, waiting for transfers between devices, per_device(): out_full = lax.all_gather(out_weight, ('batch', 'tok'), axis=0, tiled=True)  68.2 us
    all_gather x1, waiting for transfers between devices, per_device(): in_full = lax.all_gather(in_weight, ('batch', 'tok'), axis=0, tiled=True)  56.6 us
    psum x1, blocking collectives, per_device(): lax.psum((norm_grad, query_grad, key_grad), ('batch', 'tok'))  40.8 us
    unnamed x102, local copies, waits for them, and re-layouts  35.8 us
    dot_general x3, matrix products, backward_sequence(): jnp.einsum('qhd,khd->hqk', grad_out, value_block, preferred_element_type=...  24.6 us
    all_to_all x1, waiting for transfers between devices, per_device(): lax.all_to_all(grad_value_h, 'tok', split_axis=1, concat_axis=2, tiled=True)  23.7 us
    another operation x2, other arithmetic  23.5 us
  transfers between devices with their start and end apart: 12, of which 8 were waited for; matrix products, arithmetic and copies ran while one was open for 42% of the time, Pallas kernels for 0%

profile of v1, /device:TPU:0, one launch (start us, length us, event | category | flops | bytes accessed | tf_op | source)
XLA Modules:
  0.0 838.2 jit_solution(3552095954925895543)
XLA Ops:
  13.2 68.2 %all-gather.5.cloned.1.call-done = bf16[3840,768]{1,0:T(8,128)(2,1)} async-done(((bf16[120,768]{1,0:T(8,128)(2,1)}), bf16[3840,768]{1,0:T(8,128)(2,1)}) %all-gather.5.cloned.1.call-update) | async-done | bytes 5898256 | tf_op jit(solution)/shard_map/all_gather | solution.py:115
  81.4 7.4 fusion.93
  88.8 4.4 copy-done.7
  100.7 4.4 all-to-all-start.4
  105.1 56.6 %all-gather.3.cloned.1.call-done = bf16[768,5376]{1,0:T(8,128)(2,1)} async-done(((bf16[24,5376]{1,0:T(8,128)(2,1)}), bf16[768,5376]{1,0:T(8,128)(2,1)}) %all-gather.3.cloned.1.call-update) | async-done | bytes 8257552 | tf_op jit(solution)/shard_map/all_gather | solution.py:90
  161.7 8.7 %fusion.92 = f32[768,5376]{1,0:T(8,128)S(1)} fusion(bf16[768,768]{1,0:T(8,128)(2,1)S(1)} %copy-done.18, bf16[768,5376]{1,0:T(8,128)(2,1)} %all-gather.3.cloned.1.call-done), kind=kOutput, calls=%fused_computation.147 | convolution fusion | flops 6341787648 | bytes 25952256 | tf_op jit(solution)/shard_map/dot_general | solution.py:91
  170.4 5.6 copy-done.1
  183.5 4.8 fusion.91
  211.0 4.3 all-to-all-start.1
  226.3 4.9 all-to-all-done.1
  234.7 16.8 %all_gather.12 = s32[3,1024]{1,0:T(4,128)S(1)} all-gather(s32[3,256]{1,0:T(4,128)S(1)} %copy-done.37), channel_id=1, replica_groups=mesh['batch'=8,'tok'=4] {'tok'}, dimensions={1}, use_global_device_ids=true | all-gather | bytes 15360 | tf_op jit(solution)/shard_map/all_gather | solution.py:104
  265.6 45.7 %while.26 = (s32[]{:T(128)}, bf16[3,1024,3,64]{1,3,2,0:T(8,128)(2,1)}, f32[3,3,1024]{2,1,0:T(4,128)}, bf16[3,1024,3,64]{1,3,2,0:T(8,128)(2,1)}, s32[3,1024]{1,0:...) while((s32[]{:T(128)}, ...), condition=%wide.region_9.10_spmd, body=%wide.region_6.9_spmd.sunk | while | flops 845346816 | bytes 47833216 | solution.py:110
  274.5 5.7 fusion.123
  289.7 5.7 fusion.123
  305.0 5.7 fusion.123
  311.3 4.6 copy.230
  323.4 14.1 %fusion.65 = (bf16[768,3072]{1,0:T(8,128)(2,1)}, bf16[768,3072]{1,0:T(8,128)(2,1)}) fusion(f32[768,3840]{1,0:T(8,128)} %copy-done.7, f32[768,5376]{1,0:T(8,128)} %copy-done.1), kind=kLoop, calls=%fused_computation.76 | loop fusion | flops 51904512 | bytes 28311552 | tf_op jit(solution)/shard_map/convert.17
  349.1 11.8 %fusion.66 = f32[3840,768]{1,0:T(8,128)} fusion(bf16[768,768]{1,0:T(8,128)(2,1)S(1)} %copy-done.23, bf16[768,3072]{1,0:T(8,128)(2,1)} %get-tuple-element.157, bf16[768,768]{1,0:T(8,128)(2,1)S(1)} %copy.232), kind=kOutput, calls=%fused_computation.80 | convolution fusion | flops 4541644800 | bytes 18874368 | tf_op jit(solution)/shard_map/dot_general | solution.py:172
  364.6 83.9 %while.27 = (s32[]{:T(128)}, bf16[3,1024,3,64]{1,3,2,0:T(8,128)(2,1)}, bf16[3,1024,3,64]{1,3,2,0:T(8,128)(2,1)}, bf16[3,1024,3,64]{1,3,2,0:T(8,128)(2,1)}, bf16[...) while((s32[]{:T(128)}, ...), condition=%wide.region_12.13_spmd, body=%wide.region_10.12_spmd.sunk | while | flops 2063529984 | bytes 102616192 | solution.py:132
  368.1 8.2 multiply_reduce_fusion.11
  376.4 7.5 multiply_convert_fusion.7
  388.6 4.4 fusion.135
  396.4 8.2 multiply_reduce_fusion.11
  404.6 6.9 multiply_convert_fusion.7
  416.3 4.3 fusion.135
  424.0 8.2 multiply_reduce_fusion.11
  432.2 7.1 multiply_convert_fusion.7
  444.1 4.4 fusion.135
  448.5 4.6 copy.265
  461.2 23.7 %all-to-all-done.7 = bf16[4,2,73728]{2,1,0:T(2,128)(2,1)S(1)} async-done(((bf16[4,2,73728]{2,1,0:T(2,128)(2,1)}), bf16[4,2,73728]{2,1,0:T(2,128)(2,1)S(1)}, u32[]{:S(2)}, u32[]{:S(2)}) %all-to-all-start.7) | async-done | bytes 1179680 | tf_op jit(solution)/shard_map/all_to_all | solution.py:143
  489.3 4.6 copy.250
  497.0 9.9 %all-to-all-done.5 = bf16[4,3,256,3,64]{2,4,3,1,0:T(8,128)(2,1)} async-done(((bf16[4,3,256,3,64]{2,4,3,1,0:T(8,128)(2,1)}), bf16[4,3,256,3,64]{2,4,3,1,0:T(8,128)(2,1)}, u32[]{:S(2)}, u32[]{:S(2)}) %all-to-all-start.5) | async-done | bytes 1179680 | tf_op jit(solution)/shard_map/all_to_all | solution.py:137
  506.9 4.7 all-to-all-start.6
  511.8 7.8 reshape.409
  519.7 5.5 reshape.411
  527.4 6.3 copy.245
  539.3 6.6 copy.260
  569.3 4.7 copy.280
  574.0 7.7 reshape.408
  591.9 4.9 multiply_reduce_fusion.1
  606.3 4.9 copy.283
  611.2 7.8 reshape.410
  619.0 9.4 %multiply_convert_fusion.5 = (bf16[768,768]{1,0:T(8,128)(2,1)S(1)}, bf16[768,768]{1,0:T(8,128)(2,1)S(1)}) fusion(f32[768,768]{1,0:T(8,128)S(1)} %copy-done.8, f32[768,768]{1,0:T(8,128)} %copy.248, f32[768,768]{1,0:T(8,128)} %copy.241, f32[768,768]{1,0:T(8,128)} %copy.240, f32[768,768]{1,0:T(8,128)} %reshape.408, f32[768]{0:T(1024)S(1)} %mul.317, ...), kind=kLoop, calls=%fused_computation.114 | loop fusion | flops 9437184 | bytes 30676992 | tf_op jit(solution)/shard_map/convert.14
  629.4 12.1 %fusion.85 = f32[768,5376]{1,0:T(8,128)} fusion(bf16[768,768]{1,0:T(8,128)(2,1)S(1)} %copy-done.19, bf16[768,3072]{1,0:T(8,128)(2,1)} %get-tuple-element.156, bf16[768,768]{1,0:T(8,128)(2,1)S(1)} %copy-done.24, bf16[768,768]{1,0:T(8,128)(2,1)S(1)} %get-tuple-element.155, bf16[768,768]{1,0:T(8,128)(2,1)S(1)} %get-tuple-element.154), kind=kOutput, calls=%fused_computation.122 | convolution fusion | flops 6374817792 | bytes 25952256 | tf_op jit(solution)/shard_map/dot_general | solution.py:179
  642.8 13.4 %fusion.82 = (f32[768]{0:T(1024)}, f32[768]{0:T(1024)}, f32[768]{0:T(1024)}, f32[768,768]{1,0:T(8,128)}) fusion(bf16[3,256,768]{2,1,0:T(8,128)(2,1)S(1)} %copy-done.6, f32[768]{0:T(1024)S(1)} %copy-done.36, f32[768]{0:T(1024)S(1)} %copy-done.34, f32[768]{0:T(1024)S(1)} %copy-done.39, bf16[768,5376]{1,0:T(8,128)(2,1)} %all-gather.3.cloned.1.call-done, ...), kind=kOutput, calls=%fused_computation.105 | convolution fusion | flops 6380123136 | bytes 20072448 | tf_op jit(solution)/shard_map/dot_general | solution.py:167
  656.1 40.8 %all-reduce = (f32[768]{0:T(1024)}, f32[64]{0:T(128)}, f32[64]{0:T(128)}) all-reduce(f32[768]{0:T(1024)} %get-tuple-element.108, f32[64]{0:T(128)} %get-tuple-element.106, f32[64]{0:T(128)} %get-tuple-element.104), channel_id=1, replica_groups=mesh['batch'=8,'tok'=4] {'batch','tok'}, use_global_device_ids=true, to_apply=%region_20.21 | all-reduce | flops 896 | bytes 7168 | tf_op jit(solution)/shard_map/psum | solution.py:185
  702.1 9.9 %fusion.84 = bf16[768,768]{1,0:T(8,128)(2,1)} fusion(bf16[3,256,768]{2,1,0:T(8,128)(2,1)S(1)} %copy-done.6, bf16[3840,768]{1,0:T(8,128)(2,1)} %all-gather.5.cloned.1.call-done, bf16[768,3072]{1,0:T(8,128)(2,1)} %get-tuple-element.157, bf16[768,768]{1,0:T(8,128)(2,1)S(1)} %copy-done.21, f32[768]{0:T(1024)S(1)} %copy-done.32), kind=kOutput, calls=%fused_computation.107 | convolution fusion | flops 4544004096 | bytes 14158848 | tf_op jit(solution)/shard_map/dot_general | solution.py:116
  712.0 119.5 %reduce-scatter.3.cloned.1.call-done = f32[24,5376]{1,0:T(8,128)} async-done(((f32[768,5376]{1,0:T(8,128)}), f32[24,5376]{1,0:T(8,128)}) %reduce-scatter.3.cloned.1.call-update) | async-done | bytes 516112 | tf_op jit(solution)/shard_map/reduce_scatter | solution.py:178
  (256 shorter events, 221.4 us)
Async XLA Ops:
  7.2 3.8 copy-start.5
  7.2 4.2 copy-start.12
  7.2 74.2 %all-gather.5.cloned.1.call-start = ((), (), s32[]{:S(2)}) async-start(), calls=%async_computation.11 | async-start | bytes 6082560 | tf_op jit(solution)/shard_map/all_gather | solution.py:115
  7.9 153.7 %all-gather.3.cloned.1.call-start = ((), (), s32[]{:S(2)}) async-start(), calls=%async_computation.10 | async-start | bytes 8515584 | tf_op jit(solution)/shard_map/all_gather | solution.py:90
  11.8 77.1 %copy-start.22 = (bf16[768,768]{1,0:T(8,128)(2,1)}, bf16[768,768]{1,0:T(8,128)(2,1)S(1)}, u32[]{:S(2)}) copy-start(bf16[768,768]{1,0:T(8,128)(2,1)S(1)} %fusion.68) | copy-start | bytes 3538948
  88.8 4.4 copy-start.7
  100.7 61.0 %copy-start.18 = (bf16[768,768]{1,0:T(8,128)(2,1)S(1)}, bf16[768,768]{1,0:T(8,128)(2,1)}, u32[]{:S(2)}) copy-start(bf16[768,768]{1,0:T(8,128)(2,1)} %fusion.76) | copy-start | bytes 3538948
  100.7 90.5 %all-to-all-start.4 = ((bf16[3,256,12,64]{1,3,0,2:T(8,128)(2,1)}), bf16[3,256,12,64]{1,3,0,2:T(8,128)(2,1)}, u32[]{:S(2)}, u32[]{:S(2)}) async-start(bf16[3,256,12,64]{1,3,0,2:T(8,128)(2,1)} %copy.234), calls=%async_computation.4 | async-start | bytes 2359296 | tf_op jit(solution)/shard_map/all_to_all | solution.py:131
  170.4 5.6 copy-start.1
  191.2 19.8 %all-to-all-start = ((bf16[3,256,12,64]{1,3,0,2:T(8,128)(2,1)}), bf16[3,256,12,64]{1,3,0,2:T(8,128)(2,1)S(1)}, u32[]{:S(2)}, u32[]{:S(2)}) async-start(bf16[3,256,12,64]{1,3,0,2:T(8,128)(2,1)} %copy.217), calls=%async_computation | async-start | bytes 2359296 | tf_op jit(solution)/shard_map/all_to_all | solution.py:108
  199.4 2.6 copy-start.40
  202.0 3.0 copy-start.25
  211.0 20.2 %all-to-all-start.1 = ((bf16[3,256,12,64]{1,3,0,2:T(8,128)(2,1)}), bf16[3,256,12,64]{1,3,0,2:T(8,128)(2,1)}, u32[]{:S(2)}, u32[]{:S(2)}) async-start(bf16[3,256,12,64]{1,3,0,2:T(8,128)(2,1)} %copy.222), calls=%async_computation.1 | async-start | bytes 2359296 | tf_op jit(solution)/shard_map/all_to_all | solution.py:106
  219.5 2.6 copy-start.42
  222.1 3.0 copy-start.27
  225.0 9.7 %copy-start.37 = (s32[3,256]{1,0:T(4,128)S(1)}, s32[3,256]{1,0:T(4,128)}, u32[]{:S(2)}) copy-start(s32[3,256]{1,0:T(4,128)} %param.13) | copy-start | bytes 9220
  231.2 30.7 %all-to-all-start.2 = ((bf16[3,256,12,64]{1,3,0,2:T(8,128)(2,1)}), bf16[3,256,12,64]{1,3,0,2:T(8,128)(2,1)S(1)}, u32[]{:S(2)}, u32[]{:S(2)}) async-start(bf16[3,256,12,64]{1,3,0,2:T(8,128)(2,1)} %copy.227), calls=%async_computation.2 | async-start | bytes 2359296 | tf_op jit(solution)/shard_map/all_to_all | solution.py:107
  266.4 4.3 copy-start
  281.6 4.3 copy-start
  296.8 4.3 copy-start
  318.9 20.2 %all-to-all-start.3 = ((bf16[4,2,73728]{2,1,0:T(2,128)(2,1)}), bf16[4,2,73728]{2,1,0:T(2,128)(2,1)}, u32[]{:S(2)}, u32[]{:S(2)}) async-start(bf16[4,2,73728]{2,1,0:T(2,128)(2,1)} %reshape.412), calls=%async_computation.3 | async-start | bytes 2359296 | tf_op jit(solution)/shard_map/all_to_all | solution.py:113
  323.2 388.8 %reduce-scatter.5.cloned.1.call-start = ((), (), s32[]{:S(2)}) async-start(), calls=%async_computation.13 | async-start | bytes 12165120 | tf_op jit(solution)/shard_map/reduce_scatter | solution.py:171
  349.1 11.8 %copy-start.20 = (bf16[768,768]{1,0:T(8,128)(2,1)}, bf16[768,768]{1,0:T(8,128)(2,1)S(1)}, u32[]{:S(2)}) copy-start(bf16[768,768]{1,0:T(8,128)(2,1)S(1)} %copy.232) | copy-start | bytes 3538948
  361.0 3.6 copy-start.2
  361.0 3.6 copy-start.3
  361.0 3.6 copy-start.10
  456.2 3.7 copy-start.11
  456.2 28.8 %all-to-all-start.7 = ((bf16[4,2,73728]{2,1,0:T(2,128)(2,1)}), bf16[4,2,73728]{2,1,0:T(2,128)(2,1)S(1)}, u32[]{:S(2)}, u32[]{:S(2)}) async-start(bf16[4,2,73728]{2,1,0:T(2,128)(2,1)} %reshape.414), calls=%async_computation.7 | async-start | bytes 2359296 | tf_op jit(solution)/shard_map/all_to_all | solution.py:143
  485.0 4.3 copy-start.14
  485.0 21.9 %all-to-all-start.5 = ((bf16[4,3,256,3,64]{2,4,3,1,0:T(8,128)(2,1)}), bf16[4,3,256,3,64]{2,4,3,1,0:T(8,128)(2,1)}, u32[]{:S(2)}, u32[]{:S(2)}) async-start(bf16[4,3,256,3,64]{2,4,3,1,0:T(8,128)(2,1)} %pad_maximum_fusion.8), calls=%async_computation.5 | async-start | bytes 2359296 | tf_op jit(solution)/shard_map/all_to_all | solution.py:137
  493.9 17.7 %copy-start.41 = (f32[64]{0:T(128)S(1)}, f32[64]{0:T(128)}, u32[]{:S(2)}) copy-start(f32[64]{0:T(128)} %param.16) | copy-start | bytes 772
  493.9 17.8 %copy-start.43 = (f32[64]{0:T(128)S(1)}, f32[64]{0:T(128)}, u32[]{:S(2)}) copy-start(f32[64]{0:T(128)} %param.17) | copy-start | bytes 772
  506.9 74.9 %all-to-all-start.6 = ((bf16[4,2,73728]{2,1,0:T(2,128)(2,1)}), bf16[4,2,73728]{2,1,0:T(2,128)(2,1)}, u32[]{:S(2)}, u32[]{:S(2)}) async-start(bf16[4,2,73728]{2,1,0:T(2,128)(2,1)} %reshape.416), calls=%async_computation.6 | async-start | bytes 2359296 | tf_op jit(solution)/shard_map/all_to_all | solution.py:142
  511.6 319.9 %reduce-scatter.3.cloned.1.call-start = ((), (), s32[]{:S(2)}) async-start(), calls=%async_computation.12 | async-start | bytes 17031168 | tf_op jit(solution)/shard_map/reduce_scatter | solution.py:178
  511.8 7.8 copy-start.26
  511.8 7.9 copy-start.15
  511.8 7.9 copy-start.4
  519.7 5.5 copy-start.28
  519.7 5.5 copy-start.16
  556.9 3.3 copy-start.9
  589.0 2.9 copy-start.29
  589.0 2.9 copy-start.30
  611.2 7.8 copy-start.8
  619.0 10.5 %copy-start.19 = (bf16[768,768]{1,0:T(8,128)(2,1)S(1)}, bf16[768,768]{1,0:T(8,128)(2,1)}, u32[]{:S(2)}) copy-start(bf16[768,768]{1,0:T(8,128)(2,1)} %fusion.76) | copy-start | bytes 3538948
  619.0 10.5 %copy-start.24 = (bf16[768,768]{1,0:T(8,128)(2,1)S(1)}, bf16[768,768]{1,0:T(8,128)(2,1)}, u32[]{:S(2)}) copy-start(bf16[768,768]{1,0:T(8,128)(2,1)} %copy.267) | copy-start | bytes 3538948
  642.8 55.6 %copy-start.13 = (bf16[3,256,768]{2,1,0:T(8,128)(2,1)S(1)}, bf16[3,256,768]{2,1,0:T(8,128)(2,1)}, u32[]{:S(2)}) copy-start(bf16[3,256,768]{2,1,0:T(8,128)(2,1)} %param.14) | copy-start | bytes 3538948
  642.8 55.5 %copy-start.32 = (f32[768]{0:T(1024)S(1)}, f32[768]{0:T(1024)}, u32[]{:S(2)}) copy-start(f32[768]{0:T(1024)} %copy-done.31) | copy-start | bytes 9220
  698.3 3.7 copy-start.21
  (10 other events, 17.3 us)
Sparse Core Ops, SparseCore 0:
  10.9 70.3 all-gather.4
  84.3 77.3 all-gather.2
  361.1 155.1 reduce-scatter.4
  641.7 189.7 reduce-scatter.2
